TPU v7x, 256 devices: a whole 4x4x8 slice. The times are simulated.
256 devices in a mesh: seq: 16 (over z, x_lo), db: 16 (over x_hi, y, core).
Axes of the slice: x: 4 (x_hi: 2, x_lo: 2; x = x_hi * 2 + x_lo), y: 4, z: 8, core: 2. Of those that a mesh axis runs over, the one named last changes fastest.
Arguments:
- decoder_states: bfloat16 [16384, 4096], P('seq'), may hold values from -6 to 6
- query_weight: bfloat16 [4096, 4096], P(None, 'db'), may hold values from -0.09375 to 0.09375
- output_weight: bfloat16 [4096, 4096], P('db'), may hold values from -0.5 to 0.5
- neighbour_kv: bfloat16 [128, 128, 2, 4096], P('seq', None, None, 'db'), may hold values from -110 to 110
- neighbour_shard: int32 [256, 2], P('seq'), may hold values from 0 to 15, all different within a row; in each aligned block of 16 rows (0 to 15, 16 to 31, ...) at most 3 rows name the same one
- neighbour_entry: int32 [256, 2], P('seq'), may hold values from 0 to 7
- neighbour_count: int32 [256], P('seq'), may hold values from 1 to 2
Outputs:
- cross_out: bfloat16 [16384, 4096], P('seq', 'db')
Inputs may be any that keep to these rules, and one draw needn't show every extreme that they name: `neighbour_shard`: in each aligned block of 16 spans (the spans of one index of seq), no shard is named by more than 3 spans and one shard is named by exactly 3; the 2 neighbours of one span lie on different shards.
All inputs are finite; a program needn't handle non-finite values.
Results may differ from a plain program's by a relative error of at most 0.017.
Values may be sent and summed in bfloat16 or wider, within the bound.
A program may use at most 128 MiB of HBM per device.

v0:
```python
import math
import jax
import jax.numpy as jnp
from jax import lax
from jax.sharding import PartitionSpec as P

HD = 128
SPAN = 64
K = 2


def on_device(
    decoder_states,
    query_weight,
    output_weight,
    neighbour_kv,
    neighbour_shard,
    neighbour_entry,
    neighbour_count,
):
    tok_rows = decoder_states.shape[0]
    span_total = tok_rows // SPAN
    row_width = query_weight.shape[1]
    heads_here = row_width // HD
    ent_dev = neighbour_kv.shape[0]
    key_len = neighbour_kv.shape[1]
    queries = jnp.dot(decoder_states, query_weight, preferred_element_type=jnp.float32).astype(
        jnp.bfloat16
    )
    queries = queries.reshape(span_total, SPAN, heads_here, HD)
    owners = neighbour_shard.reshape(-1)
    entries = neighbour_entry.reshape(-1)
    item_count = owners.shape[0]
    empty_blocks = jnp.zeros((item_count,) + neighbour_kv.shape[1:], jnp.bfloat16)
    shard_rows = lax.all_gather(neighbour_kv, "seq", axis=0, tiled=True)
    shard_len = shard_rows.shape[0]
    local_idx = owners * ent_dev + entries
    inside = (local_idx >= 0) & (local_idx < shard_len)
    taken_rows = jnp.take(shard_rows, jnp.clip(local_idx, 0, shard_len - 1), axis=0)
    blocks = jnp.where(inside[:, None, None, None], taken_rows, empty_blocks)
    blocks = blocks.reshape(span_total, K, key_len, 2, heads_here, HD)
    key_rows = blocks[:, :, :, 0]
    val_rows = blocks[:, :, :, 1]
    scores = jnp.einsum(
        "cqhd,cknhd->chqkn", queries, key_rows, preferred_element_type=jnp.float32
    ) * (1.0 / math.sqrt(HD))
    live_slots = jnp.arange(K, dtype=jnp.int32)[None, :] < neighbour_count[:, None]
    masked = live_slots[:, None, None, :, None]
    scores = jnp.where(masked, scores, -1e30)
    top_score = jnp.max(scores, axis=(3, 4), keepdims=True)
    exponent = jnp.where(masked, jnp.exp(scores - top_score), 0.0)
    probs_bf = (exponent / jnp.sum(exponent, axis=(3, 4), keepdims=True)).astype(jnp.bfloat16)
    context = jnp.einsum(
        "chqkn,cknhd->cqhd", probs_bf, val_rows, preferred_element_type=jnp.float32
    )
    context = context.astype(jnp.bfloat16).reshape(tok_rows, row_width)
    partial_value = jnp.dot(context, output_weight, preferred_element_type=jnp.float32)
    return lax.psum_scatter(
        partial_value.astype(jnp.bfloat16), "db", scatter_dimension=1, tiled=True
    )


def solution(mesh):
    in_specs = (
        P("seq", None),
        P(None, "db"),
        P("db", None),
        P("seq", None, None, "db"),
        P("seq", None),
        P("seq", None),
        P("seq"),
    )
    out_specs = P("seq", "db")
    return jax.shard_map(
        on_device, mesh=mesh, in_specs=in_specs, out_specs=out_specs, check_vma=False
    )
```

profile of v0, /device:TPU:1, one launch (start us, length us, event | category | flops | bytes accessed | tf_op | source)
XLA Modules:
  0.0 518.9 jit_solution(15466624254692914322)
XLA Ops:
  6.5 0.0 copy-start
  6.5 0.0 copy-start.2
  6.5 0.0 copy-start.1
  6.5 0.0 all-gather.2.cloned.1.call-start
  6.5 2.5 copy.28
  9.1 0.0 all-gather.2.cloned.1.call-update
  9.1 0.0 reduce-scatter.2.cloned.1.call-start
  9.1 0.0 copy-done.2
  9.1 0.0 copy-done.1
  9.2 0.1 copy.29
  9.3 0.1 min.12
  9.3 0.1 copy.26
  9.4 0.1 copy.27
  9.5 0.0 copy-start.3
  9.5 6.3 %convolution_convert_fusion.1 = bf16[1024,256]{1,0:T(8,128)(2,1)S(1)} fusion(bf16[1024,4096]{1,0:T(8,128)(2,1)} %param.7, bf16[4096,256]{1,0:T(8,128)(2,1)} %param.8), kind=kOutput, calls=%fused_computation.13 | convolution fusion | flops 2147745792 | bytes 11010048 | tf_op jit(solution)/shard_map/dot_general | solution.py:27
  15.9 0.1 reshape.92
  16.0 0.0 copy-done.3
  16.0 0.1 iota_compare_fusion
  16.1 347.9 %all-gather.2.cloned.1.call-done = bf16[128,128,2,256]{3,1,2,0:T(8,128)(2,1)} async-done(((bf16[8,128,2,256]{3,1,2,0:T(8,128)(2,1)}), bf16[128,128,2,256]{3,1,2,0:T(8,128)(2,1)}) %all-gather.2.cloned.1.call-update) | async-done | bytes 16777232 | tf_op jit(solution)/shard_map/all_gather | solution.py:35
  364.0 8.5 %gather_fusion = bf16[32,128,2,256]{3,1,2,0:T(8,128)(2,1)} fusion(bf16[128,128,2,256]{3,1,2,0:T(8,128)(2,1)} %all-gather.2.cloned.1.call-done, s32[1024]{0:T(1024)S(1)} %pad_clamp_fusion), kind=kCustom, calls=%fused_computation | custom fusion | bytes 8388736 | tf_op jit(solution)/shard_map/jit(_take)/gather | solution.py:39
  372.5 6.5 %copy.30 = bf16[32,128,2,256]{1,3,2,0:T(8,128)(2,1)} copy(bf16[32,128,2,256]{3,1,2,0:T(8,128)(2,1)} %gather_fusion) | data formatting | bytes 8388608 | tf_op jit(solution)/shard_map/jit(_take)/gather | solution.py:39
  379.0 6.2 %copy.31 = bf16[16,2,128,2,2,128]{5,2,1,4,0,3:T(8,128)(2,1)} copy(bf16[16,2,128,2,2,128]{2,5,4,3,1,0:T(8,128)(2,1)} %bitcast.35) | data formatting | bytes 8388608 | tf_op jit(solution)/shard_map/jit(_take)/gather | solution.py:39
  385.2 2.9 select_select_fusion
  388.1 1.0 fusion.2
  389.1 1.2 fusion.3
  390.3 1.1 fusion.6
  391.4 0.5 copy.33
  391.9 0.0 copy-done
  391.9 5.6 %convolution_convert_fusion = bf16[1024,4096]{1,0:T(8,128)(2,1)} fusion(bf16[256,4096]{1,0:T(8,128)(2,1)S(1)} %copy-done, bf16[128,8,2,128]{3,2,1,0:T(2,128)(2,1)S(1)} %bitcast.36), kind=kOutput, calls=%fused_computation.1 | convolution fusion | flops 2151677952 | bytes 11010048 | tf_op jit(solution)/shard_map/dot_general | solution.py:57
  397.5 0.0 reduce-scatter.2.cloned.1.call-update
  397.5 114.5 %reduce-scatter.2.cloned.1.call-done = bf16[1024,256]{1,0:T(8,128)(2,1)} async-done(((bf16[1024,4096]{1,0:T(8,128)(2,1)}), bf16[1024,256]{1,0:T(8,128)(2,1)}) %reduce-scatter.2.cloned.1.call-update) | async-done | bytes 524304 | tf_op jit(solution)/shard_map/reduce_scatter | solution.py:58
  (3 shorter events, 0.0 us)
Async XLA Ops:
  6.5 385.4 %copy-start = (bf16[256,4096]{1,0:T(8,128)(2,1)S(1)}, bf16[256,4096]{1,0:T(8,128)(2,1)}, u32[]{:S(2)}) copy-start(bf16[256,4096]{1,0:T(8,128)(2,1)} %param.9) | copy-start | bytes 6291460
  6.5 2.6 copy-start.2
  6.5 2.6 copy-start.1
  6.5 357.5 %all-gather.2.cloned.1.call-start = ((), (), s32[]{:S(2)}) async-start(), calls=%async_computation.1 | async-start | bytes 17825792 | tf_op jit(solution)/shard_map/all_gather | solution.py:35
  9.1 502.9 %reduce-scatter.2.cloned.1.call-start = ((), (), s32[]{:S(2)}) async-start(), calls=%async_computation.2 | async-start | bytes 8912896 | tf_op jit(solution)/shard_map/reduce_scatter | solution.py:58
  9.5 6.5 %copy-start.3 = (s32[16]{0:T(128)S(1)}, s32[16]{0:T(128)}, u32[]{:S(2)}) copy-start(s32[16]{0:T(128)} %param.13) | copy-start | bytes 196
Sparse Core Ops, SparseCore 0:
  9.2 354.7 all-gather.1
  397.6 114.3 reduce-scatter.1
where the time goes:
time: 519 us
  waiting for transfers between devices  462 us (89%)
  local copies, waits for them, and re-layouts  24.8 us (5%)
  matrix products  13.9 us (3%)
  between operations  13.5 us (3%)
    all_gather x1, waiting for transfers between devices, on_device(): shard_rows = lax.all_gather(neighbour_kv, 'seq', axis=0, tiled=True)  348 us
    reduce_scatter x1, waiting for transfers between devices, on_device(): lax.psum_scatter(partial_value.astype(jnp.bfloat16), 'db', scatter_dimens...  114 us
    gather x3, local copies, waits for them, and re-layouts, on_device(): jnp.take(shard_rows, jnp.clip(local_idx, 0, shard_len - 1), axis=0)  21.2 us
  transfers between devices with their start and end apart: 2, of which 2 were waited for; matrix products, arithmetic and copies ran while one was open for 1% of the time, Pallas kernels for 0%

commit v1 on v0

--- a/solution.py
+++ b/solution.py
@@ -32,7 +32,9 @@
     entries = neighbour_entry.reshape(-1)
     item_count = owners.shape[0]
     empty_blocks = jnp.zeros((item_count,) + neighbour_kv.shape[1:], jnp.bfloat16)
-    shard_rows = lax.all_gather(neighbour_kv, "seq", axis=0, tiled=True)
+    shard_rows = jnp.concatenate(
+        lax.all_to_all(jnp.stack([neighbour_kv] * lax.axis_size("seq")), "seq", 0, 0), axis=0
+    )
     shard_len = shard_rows.shape[0]
     local_idx = owners * ent_dev + entries
     inside = (local_idx >= 0) & (local_idx < shard_len)

time: 519 us -> 557 us (1.073)
  waiting for transfers between devices: 462 us -> 485 us
  starting transfers between devices: 0.04 us -> 10.3 us
    all_to_all x0 -> x1, waiting for transfers between devices: none -> 375 us  [on_device(): lax.all_to_all(jnp.stack([neighbour_kv] * lax.axis_size('seq')), 'seq', 0...]
    all_gather x1 -> x0, waiting for transfers between devices: 348 us -> none  [on_device(): shard_rows = lax.all_gather(neighbour_kv, 'seq', axis=0, tiled=True)]
    all_to_all x0 -> x1, starting transfers between devices: none -> 10.2 us  [on_device(): lax.all_to_all(jnp.stack([neighbour_kv] * lax.axis_size('seq')), 'seq', 0...]
    another operation x0 -> x1, local copies, waits for them, and re-layouts: none -> 5.98 us  [on_device(): jnp.stack([neighbour_kv] * lax.axis_size('seq'))]
where the time goes in v1:
time: 557 us; the launch traced here: 556 us
  waiting for transfers between devices  485 us (87%)
  local copies, waits for them, and re-layouts  29.8 us (5%)
  matrix products  13.9 us (2%)
  between operations  13.5 us (2%)
  starting transfers between devices  10.3 us (2%)
    all_to_all x1, waiting for transfers between devices, on_device(): lax.all_to_all(jnp.stack([neighbour_kv] * lax.axis_size('seq')), 'seq', 0...  375 us
    reduce_scatter x1, waiting for transfers between devices, on_device(): lax.psum_scatter(partial_value.astype(jnp.bfloat16), 'db', scatter_dimens...  109 us
    gather x3, local copies, waits for them, and re-layouts, on_device(): jnp.take(shard_rows, jnp.clip(local_idx, 0, shard_len - 1), axis=0)  21.2 us
  transfers between devices with their start and end apart: 2, of which 2 were waited for; matrix products, arithmetic and copies ran while one was open for 1% of the time, Pallas kernels for 0%

profile of v1, /device:TPU:1, one launch (start us, length us, event | category | flops | bytes accessed | tf_op | source)
XLA Modules:
  0.0 556.3 jit_solution(2814450634607525181)
XLA Ops:
  6.5 0.0 copy-start
  6.5 1.5 copy.20
  8.1 6.0 %stack.2 = bf16[16,8,128,2,256]{4,2,3,1,0:T(8,128)(2,1)} broadcast(bf16[8,128,2,256]{3,1,2,0:T(8,128)(2,1)S(1)} %copy.20), dimensions={1,2,3,4} | broadcast | bytes 17825792 | tf_op jit(solution)/shard_map/stack | solution.py:36
  14.1 0.0 copy-start.1
  14.1 0.0 copy-start.2
  14.1 10.2 %all-to-all-start = ((bf16[16,8,128,2,256]{4,2,3,1,0:T(8,128)(2,1)}), bf16[16,8,128,2,256]{4,2,3,1,0:T(8,128)(2,1)}, u32[]{:S(2)}, u32[]{:S(2)}) async-start(bf16[16,8,128,2,256]{4,2,3,1,0:T(8,128)(2,1)} %stack.2), calls=%async_computation | async-start | bytes 33554432 | tf_op jit(solution)/shard_map/all_to_all | solution.py:36
  24.3 0.0 reduce-scatter.2.cloned.1.call-start
  24.4 0.0 copy-done.1
  24.4 0.0 copy-done.2
  24.4 0.1 copy.21
  24.5 0.1 min.12
  24.6 0.1 copy.19
  24.7 0.1 copy.18
  24.8 0.0 copy-start.3
  24.8 6.3 %convolution_convert_fusion.1 = bf16[1024,256]{1,0:T(8,128)(2,1)S(1)} fusion(bf16[1024,4096]{1,0:T(8,128)(2,1)} %param.7, bf16[4096,256]{1,0:T(8,128)(2,1)} %param.8), kind=kOutput, calls=%fused_computation.13 | convolution fusion | flops 2147745792 | bytes 11010048 | tf_op jit(solution)/shard_map/dot_general | solution.py:27
  31.1 0.1 reshape.98
  31.2 0.0 copy-done.3
  31.3 0.1 iota_compare_fusion
  31.3 375.5 %all-to-all-done = bf16[16,8,128,2,256]{4,2,3,1,0:T(8,128)(2,1)} async-done(((bf16[16,8,128,2,256]{4,2,3,1,0:T(8,128)(2,1)}), bf16[16,8,128,2,256]{4,2,3,1,0:T(8,128)(2,1)}, u32[]{:S(2)}, u32[]{:S(2)}) %all-to-all-start) | async-done | bytes 16777248 | tf_op jit(solution)/shard_map/all_to_all | solution.py:36
  406.8 8.5 %gather_fusion = bf16[32,128,2,256]{3,1,2,0:T(8,128)(2,1)} fusion(bf16[128,128,2,256]{3,1,2,0:T(8,128)(2,1)} %bitcast, s32[1024]{0:T(1024)S(1)} %pad_clamp_fusion), kind=kCustom, calls=%fused_computation | custom fusion | bytes 8388736 | tf_op jit(solution)/shard_map/jit(_take)/gather | solution.py:41
  415.3 6.5 %copy.22 = bf16[32,128,2,256]{1,3,2,0:T(8,128)(2,1)} copy(bf16[32,128,2,256]{3,1,2,0:T(8,128)(2,1)} %gather_fusion) | data formatting | bytes 8388608 | tf_op jit(solution)/shard_map/jit(_take)/gather | solution.py:41
  421.8 6.2 %copy.23 = bf16[16,2,128,2,2,128]{5,2,1,4,0,3:T(8,128)(2,1)} copy(bf16[16,2,128,2,2,128]{2,5,4,3,1,0:T(8,128)(2,1)} %bitcast.36) | data formatting | bytes 8388608 | tf_op jit(solution)/shard_map/jit(_take)/gather | solution.py:41
  428.0 2.9 select_select_fusion
  430.9 1.0 fusion.2
  431.9 1.2 fusion.3
  433.1 1.1 fusion.6
  434.2 0.5 copy.25
  434.7 0.0 copy-done
  434.7 5.6 %convolution_convert_fusion = bf16[1024,4096]{1,0:T(8,128)(2,1)} fusion(bf16[256,4096]{1,0:T(8,128)(2,1)S(1)} %copy-done, bf16[128,8,2,128]{3,2,1,0:T(2,128)(2,1)S(1)} %bitcast.37), kind=kOutput, calls=%fused_computation.1 | convolution fusion | flops 2151677952 | bytes 11010048 | tf_op jit(solution)/shard_map/dot_general | solution.py:59
  440.3 0.0 reduce-scatter.2.cloned.1.call-update
  440.3 109.1 %reduce-scatter.2.cloned.1.call-done = bf16[1024,256]{1,0:T(8,128)(2,1)} async-done(((bf16[1024,4096]{1,0:T(8,128)(2,1)}), bf16[1024,256]{1,0:T(8,128)(2,1)}) %reduce-scatter.2.cloned.1.call-update) | async-done | bytes 524304 | tf_op jit(solution)/shard_map/reduce_scatter | solution.py:60
  (3 shorter events, 0.0 us)
Async XLA Ops:
  6.5 428.2 %copy-start = (bf16[256,4096]{1,0:T(8,128)(2,1)S(1)}, bf16[256,4096]{1,0:T(8,128)(2,1)}, u32[]{:S(2)}) copy-start(bf16[256,4096]{1,0:T(8,128)(2,1)} %param.9) | copy-start | bytes 6291460
  14.1 10.3 %copy-start.1 = (s32[16,2]{0,1:T(2,128)S(1)}, s32[16,2]{0,1:T(2,128)}, u32[]{:S(2)}) copy-start(s32[16,2]{0,1:T(2,128)} %param.12) | copy-start | bytes 388
  14.1 10.3 %copy-start.2 = (s32[16,2]{0,1:T(2,128)S(1)}, s32[16,2]{0,1:T(2,128)}, u32[]{:S(2)}) copy-start(s32[16,2]{0,1:T(2,128)} %param.11) | copy-start | bytes 388
  14.1 392.7 %all-to-all-start = ((bf16[16,8,128,2,256]{4,2,3,1,0:T(8,128)(2,1)}), bf16[16,8,128,2,256]{4,2,3,1,0:T(8,128)(2,1)}, u32[]{:S(2)}, u32[]{:S(2)}) async-start(bf16[16,8,128,2,256]{4,2,3,1,0:T(8,128)(2,1)} %stack.2), calls=%async_computation | async-start | bytes 33554432 | tf_op jit(solution)/shard_map/all_to_all | solution.py:36
  24.3 525.1 %reduce-scatter.2.cloned.1.call-start = ((), (), s32[]{:S(2)}) async-start(), calls=%async_computation.2 | async-start | bytes 8912896 | tf_op jit(solution)/shard_map/reduce_scatter | solution.py:60
  24.8 6.5 %copy-start.3 = (s32[16]{0:T(128)S(1)}, s32[16]{0:T(128)}, u32[]{:S(2)}) copy-start(s32[16]{0:T(128)} %param.13) | copy-start | bytes 196
Sparse Core Ops, SparseCore 0:
  440.4 108.9 reduce-scatter.1
